TPU v7x, 32 devices: a whole 2x2x4 slice. The times are simulated.
32 devices in a mesh: row: 4 (over y, x), col: 2 (over core), dp: 4 (over z).
Axes of the slice: x: 2, y: 2, z: 4, core: 2. Of those that a mesh axis runs over, the one named last changes fastest.
Arguments:
- out_grad: bfloat16 [4, 128, 4096], P('dp', 'col', 'row'), may hold values from -6 to 6
- saved_hidden: bfloat16 [4, 128, 14336], P('dp', 'row', 'col'), may hold values from -6 to 6
- down_weight: bfloat16 [14336, 4096], P(('col', 'dp'), 'row'), may hold values from -0.046875 to 0.046875
Outputs:
- hidden_grad: bfloat16 [4, 128, 14336], P('dp', 'row', 'col')
- weight_grad: bfloat16 [14336, 4096], P(('col', 'dp'), 'row')
All inputs are finite; a program needn't handle non-finite values.
Results may differ from a plain program's by a relative error of at most 0.009.
Values may be sent and summed in bfloat16 or wider, within the bound.
A program may use at most 64 MiB of HBM per device.

v0:
```python
import jax
import jax.numpy as jnp
from jax import lax
from jax.sharding import PartitionSpec as P


def on_device(out_grad, saved_hidden, down_weight):
    grad_local = out_grad[0]
    hidden_local = saved_hidden[0]
    units = down_weight.shape[0]
    width = down_weight.shape[1]
    grad_replica = lax.all_gather(grad_local, "col", axis=0, tiled=True)
    grad_all = lax.all_gather(grad_replica[:, None, :], "dp", axis=1, tiled=True)
    tok_count = grad_all.shape[0]
    replica_count = grad_all.shape[1]
    local_tokens = hidden_local.shape[0]
    hidden_units = lax.all_to_all(
        hidden_local[:, None, :], "dp", split_axis=2, concat_axis=1, tiled=True
    )
    factor = jnp.float32(1.0) / jnp.sqrt(jnp.float32(tok_count * replica_count))
    flat_grad = grad_all.reshape(tok_count * replica_count, width)
    rows = flat_grad
    summed = lax.psum_scatter(
        lax.dot_general(
            rows, down_weight, (((1,), (1,)), ((), ())), preferred_element_type=jnp.float32
        ).astype(jnp.bfloat16),
        "row",
        scatter_dimension=0,
        tiled=True,
    )
    local_grad = summed.reshape(local_tokens, replica_count, units)
    returned = lax.all_to_all(local_grad, "dp", split_axis=1, concat_axis=2, tiled=True)
    hidden_grad = returned.reshape(1, local_tokens, -1)
    rows = grad_all
    left = lax.all_gather(hidden_units, "row", axis=0, tiled=True).reshape(-1, units)
    right = rows.reshape(-1, width)
    total = lax.dot_general(
        left, right, (((0,), (0,)), ((), ())), preferred_element_type=jnp.float32
    )
    weight_grad = (total * factor).astype(jnp.bfloat16)
    return (hidden_grad, weight_grad)


def solution(mesh):
    in_specs = (P("dp", "col", "row"), P("dp", "row", "col"), P(("col", "dp"), "row"))
    out_specs = (P("dp", "row", "col"), P(("col", "dp"), "row"))
    return jax.shard_map(
        on_device, mesh=mesh, in_specs=in_specs, out_specs=out_specs, check_vma=False
    )
```

profile of v0, /device:TPU:0, one launch (start us, length us, event | category | flops | bytes accessed | tf_op | source)
XLA Modules:
  0.0 169.9 jit_solution(11268376020256023476)
XLA Ops:
  7.2 0.0 all-gather.7.cloned.1.call-start
  7.2 2.3 %all-gather = bf16[1,128,1024]{2,1,0:T(8,128)(2,1)S(1)} all-gather(bf16[1,64,1024]{2,1,0:T(8,128)(2,1)} %param.3), channel_id=2, replica_groups=mesh['row'=4,'col'=2,'dp'=4] {'col'}, dimensions={1}, use_global_device_ids=true | all-gather | bytes 393216 | tf_op jit(solution)/shard_map/all_gather | solution.py:12
  9.5 0.8 copy.19
  10.4 0.0 all-gather.7.cloned.1.call-update
  10.4 0.0 reduce-scatter.2.cloned.1.call-start
  10.5 30.7 %all-gather.7.cloned.1.call-done = bf16[1,128,4096]{1,2,0:T(8,128)(2,1)} async-done(((bf16[1,128,1024]{1,2,0:T(8,128)(2,1)}), bf16[1,128,4096]{1,2,0:T(8,128)(2,1)}) %all-gather.7.cloned.1.call-update) | async-done | bytes 1048592 | tf_op jit(solution)/shard_map/all_gather | solution.py:13
  41.1 1.5 copy.20
  42.6 0.7 reshape.22
  43.3 0.0 copy-start.1
  43.3 5.4 %convolution_convert_fusion = bf16[512,1792]{1,0:T(8,128)(2,1)} fusion(bf16[512,1024]{1,0:T(8,128)(2,1)S(1)} %reshape.22, bf16[1792,1024]{1,0:T(8,128)(2,1)} %param.5), kind=kOutput, calls=%fused_computation.2 | convolution fusion | flops 1879965696 | bytes 6553600 | tf_op jit(solution)/shard_map/dot_general | solution.py:24
  48.8 0.0 reduce-scatter.2.cloned.1.call-update
  48.8 0.0 all-gather.5.cloned.1.call-start
  48.8 0.0 copy-done.1
  48.8 5.9 %copy.23 = bf16[32,1,7168]{0,1,2:T(2,128)(2,1)} copy(bf16[32,1,7168]{2,0,1:T(8,128)(2,1)S(1)} %bitcast.17) | data formatting | bytes 917504 | tf_op jit(solution)/shard_map/broadcast_in_dim;squeeze | solution.py:18
  54.8 0.5 broadcast
  55.3 39.8 %reduce = bf16[7168,32]{1,0:T(8,128)(2,1)S(1)} reduce(bf16[7168,1,32]{2,1,0:T(2,128)(2,1)} %bitcast.14, bf16[]{:T(256)} %broadcast), dimensions={1}, to_apply=%bitcast.8.reduce_sub_computation | reduce | bytes 917506
  95.1 1.8 %reshape.29 = bf16[4,2,28672]{2,1,0:T(2,128)(2,1)S(1)} reshape(bf16[7168,32]{1,0:T(8,128)(2,1)S(1)} %reduce) | data formatting | bytes 917504
  96.8 15.8 %all_to_all.21 = bf16[4,2,28672]{2,1,0:T(2,128)(2,1)S(1)} all-to-all(bf16[4,2,28672]{2,1,0:T(2,128)(2,1)S(1)} %reshape.29), channel_id=1, replica_groups=mesh['row'=4,'col'=2,'dp'=4] {'dp'}, dimensions={0} | all-to-all | bytes 917504 | tf_op jit(solution)/shard_map/all_to_all | solution.py:17
  112.7 3.0 %reshape.30 = bf16[7168,1,32]{2,1,0:T(2,128)(2,1)} reshape(bf16[4,2,28672]{2,1,0:T(2,128)(2,1)S(1)} %all_to_all.21) | data formatting | bytes 917504
  115.7 7.1 %copy.24 = bf16[32,1,7168]{2,0,1:T(8,128)(2,1)S(1)} copy(bf16[32,1,7168]{0,1,2:T(2,128)(2,1)} %bitcast.15) | data formatting | bytes 917504 | tf_op jit(solution)/shard_map/all_to_all | solution.py:17
  122.8 0.3 all_to_all.8
  123.1 0.8 copy.25
  123.9 0.0 all-gather.5.cloned.1.call-update
  123.9 0.0 reduce-scatter.2.cloned.1.call-done
  124.0 1.1 reshape.23
  125.1 0.8 copy.21
  125.9 3.6 %all-to-all-start = ((bf16[32,4,1792]{2,0,1:T(8,128)(2,1)}), bf16[32,4,1792]{2,0,1:T(8,128)(2,1)S(1)}, u32[]{:S(2)}, u32[]{:S(2)}) async-start(bf16[32,4,1792]{2,0,1:T(8,128)(2,1)} %copy.21), calls=%async_computation.1 | async-start | bytes 917504 | tf_op jit(solution)/shard_map/all_to_all | solution.py:32
  129.6 26.9 %all-gather.5.cloned.1.call-done = bf16[128,4,1792]{2,0,1:T(8,128)(2,1)} async-done(((bf16[32,4,1792]{2,0,1:T(8,128)(2,1)}), bf16[128,4,1792]{2,0,1:T(8,128)(2,1)}) %all-gather.5.cloned.1.call-update) | async-done | bytes 1835024 | tf_op jit(solution)/shard_map/all_gather | solution.py:35
  156.5 5.5 %fusion = bf16[1792,1024]{1,0:T(8,128)(2,1)} fusion(bf16[128,4,1792]{2,0,1:T(8,128)(2,1)} %all-gather.5.cloned.1.call-done, bf16[128,4,1024]{0,2,1:T(8,128)(2,1)S(1)} %bitcast.16), kind=kOutput, calls=%fused_computation.1 | convolution fusion | flops 1882718208 | bytes 6553600 | tf_op jit(solution)/shard_map/dot_general | solution.py:37
  161.9 0.0 all-to-all-done
  161.9 0.4 copy.22
  162.3 1.1 reshape.24
  (2 shorter events, 0.0 us)
Async XLA Ops:
  7.2 34.0 %all-gather.7.cloned.1.call-start = ((), (), s32[]{:S(2)}) async-start(), calls=%async_computation.5 | async-start | bytes 1310720 | tf_op jit(solution)/shard_map/all_gather | solution.py:13
  10.4 113.5 %reduce-scatter.2.cloned.1.call-start = ((), (), s32[]{:S(2)}) async-start(), calls=%async_computation.3 | async-start | bytes 2293760 | tf_op jit(solution)/shard_map/reduce_scatter | solution.py:23
  43.3 5.5 %copy-start.1 = (bf16[1,32,7168]{2,1,0:T(8,128)(2,1)S(1)}, bf16[1,32,7168]{2,1,0:T(8,128)(2,1)}, u32[]{:S(2)}) copy-start(bf16[1,32,7168]{2,1,0:T(8,128)(2,1)} %param.4) | copy-start | bytes 1376260
  48.8 107.7 %all-gather.5.cloned.1.call-start = ((), (), s32[]{:S(2)}) async-start(), calls=%async_computation.4 | async-start | bytes 2293760 | tf_op jit(solution)/shard_map/all_gather | solution.py:35
  115.7 40.8 %copy-start = (bf16[1,128,4096]{1,2,0:T(8,128)(2,1)S(1)}, bf16[1,128,4096]{1,2,0:T(8,128)(2,1)}, u32[]{:S(2)}) copy-start(bf16[1,128,4096]{1,2,0:T(8,128)(2,1)} %all-gather.7.cloned.1.call-done) | copy-start | bytes 3145732
  125.9 36.0 %all-to-all-start = ((bf16[32,4,1792]{2,0,1:T(8,128)(2,1)}), bf16[32,4,1792]{2,0,1:T(8,128)(2,1)S(1)}, u32[]{:S(2)}, u32[]{:S(2)}) async-start(bf16[32,4,1792]{2,0,1:T(8,128)(2,1)} %copy.21), calls=%async_computation.1 | async-start | bytes 917504 | tf_op jit(solution)/shard_map/all_to_all | solution.py:32
Sparse Core Ops, SparseCore 0:
  10.5 30.5 all-gather.6
  48.9 32.4 reduce-scatter.1
  124.1 32.3 all-gather.4
where the time goes:
time: 170 us
  waiting for transfers between devices  57.7 us (34%)
  other arithmetic  39.8 us (23%)
  local copies, waits for them, and re-layouts  25.9 us (15%)
  blocking collectives  18.2 us (11%)
  between operations  13.8 us (8%)
  matrix products  10.9 us (6%)
  starting transfers between devices  3.77 us (2%)
    unnamed x1, other arithmetic  39.8 us
    all_gather x1, waiting for transfers between devices, on_device(): lax.all_gather(grad_replica[:, None, :], 'dp', axis=1, tiled=True)  30.7 us
    all_gather x1, waiting for transfers between devices, on_device(): lax.all_gather(hidden_units, 'row', axis=0, tiled=True).reshape(-1, units)  26.9 us
    all_to_all x1, blocking collectives, on_device(): lax.all_to_all(hidden_local[:, None, :], 'dp', split_axis=2, concat_axis=...  15.8 us
    all_to_all x3, local copies, waits for them, and re-layouts, on_device(): lax.all_to_all(hidden_local[:, None, :], 'dp', split_axis=2, concat_axis=...  8.22 us
    another operation x1, local copies, waits for them, and re-layouts, on_device(): hidden_local[:, None, :]  5.94 us
    dot_general x1, matrix products, on_device(): lax.dot_general(left, right, (((0,), (0,)), ((), ())), preferred_element_...  5.47 us
    dot_general x1, matrix products, on_device(): lax.dot_general(rows, down_weight, (((1,), (1,)), ((), ())), preferred_el...  5.43 us
  transfers between devices with their start and end apart: 4, of which 2 were waited for; matrix products, arithmetic and copies ran while one was open for 39% of the time, Pallas kernels for 0%

commit v1 on v0

--- a/solution.py
+++ b/solution.py
@@ -14,9 +14,15 @@
     tok_count = grad_all.shape[0]
     replica_count = grad_all.shape[1]
     local_tokens = hidden_local.shape[0]
-    hidden_units = lax.all_to_all(
-        hidden_local[:, None, :], "dp", split_axis=2, concat_axis=1, tiled=True
-    )
+
+    def produce_bench(point, peer_axis, out_dim, axis_k):
+        b_next = lax.psum(1, axis_name=peer_axis)
+        p_next = jnp.split(point, b_next, axis=out_dim)
+        r2 = jnp.stack(p_next)
+        part_now = lax.all_to_all(r2, axis_name=peer_axis, split_axis=0, concat_axis=0)
+        return jnp.concatenate(part_now, axis=axis_k)
+
+    hidden_units = produce_bench(hidden_local[:, None, :], "dp", 2, 1)
     factor = jnp.float32(1.0) / jnp.sqrt(jnp.float32(tok_count * replica_count))
     flat_grad = grad_all.reshape(tok_count * replica_count, width)
     rows = flat_grad

time: 170 us -> 132 us (0.78)
  other arithmetic: 39.8 us -> 0.06 us
  waiting for transfers between devices: 57.7 us -> 74.5 us
  local copies, waits for them, and re-layouts: 25.9 us -> 11.2 us
    unnamed x1 -> x0, other arithmetic: 39.8 us -> none
    reduce_scatter x1, waiting for transfers between devices: 0.02 us -> 15.4 us  [on_device(): lax.psum_scatter(lax.dot_general(rows, down_weight, (((1,), (1,)), ((), (...]
    all_to_all x3 -> x0, local copies, waits for them, and re-layouts: 8.22 us -> none  [on_device(): lax.all_to_all(hidden_local[:, None, :], 'dp', split_axis=2, concat_axis=...]
    another operation x1, local copies, waits for them, and re-layouts: 5.94 us -> 0.03 us  [produce_bench(): r2 = jnp.stack(p_next)]
    unnamed x7 -> x4, local copies, waits for them, and re-layouts: 5.28 us -> 0.01 us
    all_gather x0 -> x1, local copies, waits for them, and re-layouts: none -> 3.6 us  [on_device(): lax.all_gather(hidden_units, 'row', axis=0, tiled=True).reshape(-1, units)]
  transfers between devices with their start and end apart: 4 -> 4, of which waited for: 2 -> 3; matrix products, arithmetic and copies ran while one was open for 39% -> 8% of each run, Pallas kernels for 0% -> 0%
where the time goes in v1:
time: 132 us
  waiting for transfers between devices  74.5 us (56%)
  blocking collectives  18.1 us (14%)
  between operations  13.8 us (10%)
  local copies, waits for them, and re-layouts  11.2 us (8%)
  matrix products  9.37 us (7%)
  starting transfers between devices  4.72 us (4%)
    all_gather x1, waiting for transfers between devices, on_device(): lax.all_gather(grad_replica[:, None, :], 'dp', axis=1, tiled=True)  30.7 us
    all_gather x1, waiting for transfers between devices, on_device(): lax.all_gather(hidden_units, 'row', axis=0, tiled=True).reshape(-1, units)  28.3 us
    all_to_all x1, blocking collectives, produce_bench(): lax.all_to_all(r2, axis_name=peer_axis, split_axis=0, concat_axis=0)  15.8 us
    reduce_scatter x1, waiting for transfers between devices, on_device(): lax.psum_scatter(lax.dot_general(rows, down_weight, (((1,), (1,)), ((), (...  15.4 us
    dot_general x1, matrix products, on_device(): lax.dot_general(rows, down_weight, (((1,), (1,)), ((), ())), preferred_el...  5.43 us
    all_to_all x1, starting transfers between devices, on_device(): lax.all_to_all(local_grad, 'dp', split_axis=1, concat_axis=2, tiled=True)  4.6 us
    dot_general x1, matrix products, on_device(): lax.dot_general(left, right, (((0,), (0,)), ((), ())), preferred_element_...  3.94 us
    all_gather x1, local copies, waits for them, and re-layouts, on_device(): lax.all_gather(hidden_units, 'row', axis=0, tiled=True).reshape(-1, units)  3.6 us
  transfers between devices with their start and end apart: 4, of which 3 were waited for; matrix products, arithmetic and copies ran while one was open for 8% of the time, Pallas kernels for 0%

profile of v1, /device:TPU:0, one launch (start us, length us, event | category | flops | bytes accessed | tf_op | source)
XLA Modules:
  0.0 131.8 jit_solution(17426707782934796457)
XLA Ops:
  7.2 0.0 all-gather.6.cloned.1.call-start
  7.2 2.3 %all-gather = bf16[1,128,1024]{2,1,0:T(8,128)(2,1)S(1)} all-gather(bf16[1,64,1024]{2,1,0:T(8,128)(2,1)} %param.3), channel_id=2, replica_groups=mesh['row'=4,'col'=2,'dp'=4] {'col'}, dimensions={1}, use_global_device_ids=true | all-gather | bytes 393216 | tf_op jit(solution)/shard_map/all_gather | solution.py:12
  9.5 0.8 copy.28
  10.4 0.0 all-gather.6.cloned.1.call-update
  10.4 0.0 reduce-scatter.2.cloned.1.call-start
  10.5 30.7 %all-gather.6.cloned.1.call-done = bf16[1,128,4096]{1,2,0:T(8,128)(2,1)} async-done(((bf16[1,128,1024]{1,2,0:T(8,128)(2,1)}), bf16[1,128,4096]{1,2,0:T(8,128)(2,1)}) %all-gather.6.cloned.1.call-update) | async-done | bytes 1048592 | tf_op jit(solution)/shard_map/all_gather | solution.py:13
  41.1 1.5 %copy.29 = bf16[1,128,4096]{2,1,0:T(8,128)(2,1)S(1)} copy(bf16[1,128,4096]{1,2,0:T(8,128)(2,1)} %all-gather.6.cloned.1.call-done) | data formatting | bytes 2097152 | tf_op jit(solution)/shard_map/all_gather | solution.py:13
  42.6 0.7 reshape.25
  43.3 0.0 copy-start.1
  43.3 5.4 %convolution_convert_fusion = bf16[512,1792]{1,0:T(8,128)(2,1)} fusion(bf16[512,1024]{1,0:T(8,128)(2,1)S(1)} %reshape.25, bf16[1792,1024]{1,0:T(8,128)(2,1)} %param.5), kind=kOutput, calls=%fused_computation.2 | convolution fusion | flops 1879965696 | bytes 6553600 | tf_op jit(solution)/shard_map/dot_general | solution.py:30
  48.8 0.0 reduce-scatter.2.cloned.1.call-update
  48.8 0.0 all-gather.8.cloned.1.call-start
  48.8 0.0 copy-done.1
  48.9 0.1 pad_maximum_fusion
  49.0 15.8 %all_to_all.14 = bf16[4,32,1,1792]{3,1,2,0:T(8,128)(2,1)S(1)} all-to-all(bf16[4,32,1,1792]{3,1,2,0:T(8,128)(2,1)S(1)} %pad_maximum_fusion), channel_id=1, replica_groups=mesh['row'=4,'col'=2,'dp'=4] {'dp'}, dimensions={0} | all-to-all | bytes 917504 | tf_op jit(solution)/shard_map/all_to_all | solution.py:22
  64.8 1.1 copy.32
  65.9 0.0 copy-start
  65.9 0.0 all-gather.8.cloned.1.call-update
  65.9 15.4 %reduce-scatter.2.cloned.1.call-done = bf16[128,1792]{1,0:T(8,128)(2,1)} async-done(((bf16[512,1792]{1,0:T(8,128)(2,1)}), bf16[128,1792]{1,0:T(8,128)(2,1)}) %reduce-scatter.2.cloned.1.call-update) | async-done | bytes 458768 | tf_op jit(solution)/shard_map/reduce_scatter | solution.py:29
  81.3 1.1 reshape.26
  82.5 0.8 copy.30
  83.3 4.6 %all-to-all-start = ((bf16[32,4,1792]{2,0,1:T(8,128)(2,1)}), bf16[32,4,1792]{2,0,1:T(8,128)(2,1)S(1)}, u32[]{:S(2)}, u32[]{:S(2)}) async-start(bf16[32,4,1792]{2,0,1:T(8,128)(2,1)} %copy.30), calls=%async_computation.1 | async-start | bytes 917504 | tf_op jit(solution)/shard_map/all_to_all | solution.py:38
  87.9 28.3 %all-gather.8.cloned.1.call-done = bf16[128,4,1,1792]{3,1,2,0:T(4,128)(2,1)} async-done(((bf16[32,4,1,1792]{3,1,2,0:T(4,128)(2,1)}), bf16[128,4,1,1792]{3,1,2,0:T(4,128)(2,1)}) %all-gather.8.cloned.1.call-update) | async-done | bytes 1835024 | tf_op jit(solution)/shard_map/all_gather | solution.py:41
  116.2 3.6 %copy.33 = bf16[128,4,1,1792]{0,3,1,2:T(8,128)(2,1)S(1)} copy(bf16[128,4,1,1792]{3,1,2,0:T(4,128)(2,1)} %all-gather.8.cloned.1.call-done) | data formatting | bytes 3670016 | tf_op jit(solution)/shard_map/all_gather | solution.py:41
  119.8 0.0 copy-done
  119.8 3.9 %fusion = bf16[1792,1024]{1,0:T(8,128)(2,1)} fusion(bf16[128,4,1024]{0,2,1:T(8,128)(2,1)S(1)} %bitcast.22, bf16[128,4,1,1792]{0,3,1,2:T(8,128)(2,1)S(1)} %copy.33), kind=kOutput, calls=%fused_computation.1 | convolution fusion | flops 1882718208 | bytes 6553600 | tf_op jit(solution)/shard_map/dot_general | solution.py:43
  123.8 0.0 all-to-all-done
  123.8 0.4 copy.31
  124.2 1.1 reshape.27
  (1 shorter events, 0.0 us)
Async XLA Ops:
  7.2 34.0 %all-gather.6.cloned.1.call-start = ((), (), s32[]{:S(2)}) async-start(), calls=%async_computation.4 | async-start | bytes 1310720 | tf_op jit(solution)/shard_map/all_gather | solution.py:13
  10.4 70.9 %reduce-scatter.2.cloned.1.call-start = ((), (), s32[]{:S(2)}) async-start(), calls=%async_computation.3 | async-start | bytes 2293760 | tf_op jit(solution)/shard_map/reduce_scatter | solution.py:29
  43.3 5.5 %copy-start.1 = (bf16[1,32,7168]{2,1,0:T(8,128)(2,1)S(1)}, bf16[1,32,7168]{2,1,0:T(8,128)(2,1)}, u32[]{:S(2)}) copy-start(bf16[1,32,7168]{2,1,0:T(8,128)(2,1)} %param.4) | copy-start | bytes 1376260
  48.8 67.4 %all-gather.8.cloned.1.call-start = ((), (), s32[]{:S(2)}) async-start(), calls=%async_computation.5 | async-start | bytes 2293760 | tf_op jit(solution)/shard_map/all_gather | solution.py:41
  65.9 53.9 %copy-start = (bf16[1,128,4096]{1,2,0:T(8,128)(2,1)S(1)}, bf16[1,128,4096]{1,2,0:T(8,128)(2,1)}, u32[]{:S(2)}) copy-start(bf16[1,128,4096]{1,2,0:T(8,128)(2,1)} %all-gather.6.cloned.1.call-done) | copy-start | bytes 3145732
  83.3 40.5 %all-to-all-start = ((bf16[32,4,1792]{2,0,1:T(8,128)(2,1)}), bf16[32,4,1792]{2,0,1:T(8,128)(2,1)S(1)}, u32[]{:S(2)}, u32[]{:S(2)}) async-start(bf16[32,4,1792]{2,0,1:T(8,128)(2,1)} %copy.30), calls=%async_computation.1 | async-start | bytes 917504 | tf_op jit(solution)/shard_map/all_to_all | solution.py:38
Sparse Core Ops, SparseCore 0:
  10.5 30.5 all-gather.5
  48.9 32.3 reduce-scatter.1
  83.2 32.9 all-gather.7
